TPU v7x, 32 devices: a whole 2x2x4 slice. The times are simulated.
32 devices in a mesh: fine: 8 (over y, x, core), coarse: 4 (over z).
Axes of the slice: x: 2, y: 2, z: 4, core: 2. Of those that a mesh axis runs over, the one named last changes fastest.
Arguments:
- force: float32 [3, 131072], P(None, ('fine', 'coarse')), may hold values from -6 to 6
- inv_diag: float32 [3, 131072], P(None, ('fine', 'coarse')), may hold values from 0.01 to 0.03
- k_ref: float32 [24, 24], replicated
- coefs: float32 [65536], P(('fine', 'coarse')), may hold values from 0.5 to 2
- conn: int32 [8, 65536], P(None, ('fine', 'coarse')), may hold values from 0 to 5119
- felem: int32 [24576], P(('fine', 'coarse')), may hold values from 0 to 2047
- weights: float32 [8, 8, 24576], P(None, None, ('fine', 'coarse')), may hold values from -0.6 to 0.6
- counts: int32 [32, 32], P(('fine', 'coarse')), may hold values from 1 to 24, as said below
- celem: int32 [32, 768], P(('fine', 'coarse')), may hold values from 0 to 127
Outputs:
- smoothed: float32 [3, 131072], P(None, ('fine', 'coarse'))
- coarse_load: float32 [24, 4096], P(None, ('fine', 'coarse'))
Inputs may be any that keep to these rules, and one draw needn't show every extreme that they name: `counts`: in every draw one owner receives 24 used slots from every partition; every count is at least 1.
All inputs are finite; a program needn't handle non-finite values.
Results may differ from a plain program's by a relative error of at most 0.0003.
Values sent between devices are 32-bit elements; how exact they have to be, the bound alone decides.
A program may use at most 128 MiB of HBM per device.

v0:
```python
import jax
import jax.numpy as jnp
from jax import lax
from jax.sharding import PartitionSpec as P

BAND = 512
CAP = 24
CE_DEV = 128


LOW_END = 0.3
HIGH_END = 2.5


def with_halo(array, sides, width):
    for axis, dim in sides:
        size, length = (lax.axis_size(axis), array.shape[dim])
        up = [(i, (i + 1) % size) for i in range(size - 1)]
        down = [(j, i) for i, j in up]
        last = lax.slice_in_dim(array, length - width, length, axis=dim)
        first = lax.slice_in_dim(array, 0, width, axis=dim)
        before = lax.ppermute(last, axis, up)
        after = lax.ppermute(first, axis, down)
        array = jnp.concatenate([before, array, after], axis=dim)
    return array


def shifted(value, axis, steps):
    count = lax.axis_size(axis)
    first, last = (max(0, -steps), min(count, count - steps))
    return lax.ppermute(value, axis, [(source, source + steps) for source in range(first, last)])


def extend(field):
    return with_halo(field, ((("fine", "coarse"), 1),), BAND)


def apply_operator(field, k_ref, coefs, conn):
    wide = extend(field)
    local = wide[:, conn].reshape(24, -1)
    product = (
        jnp.dot(k_ref, local, precision=lax.Precision.HIGHEST, preferred_element_type=jnp.float32)
        * coefs[None, :]
    )
    summed = jnp.zeros(wide.shape, jnp.float32).at[:, conn].add(product.reshape(3, 8, -1))
    owned = summed[:, BAND:-BAND]
    from_upper = shifted(summed[:, :BAND], ("fine", "coarse"), -1)
    from_lower = shifted(summed[:, -BAND:], ("fine", "coarse"), 1)
    owned = owned.at[:, -BAND:].add(from_upper)
    return owned.at[:, :BAND].add(from_lower)


def on_device(force, inv_diag, k_ref, coefs, conn, felem, weights, counts, celem):
    theta = (HIGH_END + LOW_END) / 2.0
    delta = (HIGH_END - LOW_END) / 2.0
    sigma = theta / delta
    rho = 1.0 / sigma
    solution = jnp.zeros_like(force)
    resid = force
    direction = inv_diag * resid / theta
    for sweep in range(3):
        solution = solution + direction
        resid = resid - apply_operator(direction, k_ref, coefs, conn)
        if sweep < 2:
            rho_new = 1.0 / (2.0 * sigma - rho)
            direction = rho_new * rho * direction + 2.0 * rho_new / delta * inv_diag * resid
            rho = rho_new
    wide = extend(resid)
    values = wide[:, conn[:, felem]]
    contrib = jnp.einsum("ijs,cjs->cis", weights, values, precision=lax.Precision.HIGHEST)
    owners = counts.shape[1]
    per_src = felem.shape[0]
    slot_iota = jnp.arange(per_src, dtype=jnp.int32)
    live = slot_iota % CAP < jnp.repeat(counts[0], CAP)
    contrib = (contrib * live[None, None, :].astype(jnp.float32)).reshape(24, owners, CAP)
    element_iota = jnp.arange(CE_DEV, dtype=jnp.int32)
    arrived = lax.all_to_all(contrib, ("fine", "coarse"), split_axis=1, concat_axis=1, tiled=True)
    arrived = arrived.reshape(24, per_src)
    selector = (celem[0][:, None] == element_iota[None, :]).astype(jnp.float32)
    load = jnp.dot(
        arrived, selector, precision=lax.Precision.HIGHEST, preferred_element_type=jnp.float32
    )
    return (solution, load)


def solution(mesh):
    placed = (
        P(None, ("fine", "coarse")),
        P(None, ("fine", "coarse")),
        P(),
        P(("fine", "coarse")),
        P(None, ("fine", "coarse")),
        P(("fine", "coarse")),
        P(None, None, ("fine", "coarse")),
        P(("fine", "coarse"), None),
        P(("fine", "coarse"), None),
    )
    return jax.shard_map(
        on_device,
        mesh=mesh,
        in_specs=placed,
        out_specs=(P(None, ("fine", "coarse")), P(None, ("fine", "coarse"))),
        check_vma=False,
    )
```

profile of v0, /device:TPU:0, one launch (start us, length us, event | category | flops | bytes accessed | tf_op | source)
XLA Modules:
  0.0 637.7 jit_solution(10427841340992226441)
XLA Ops:
  1.6 4.9 collective-permute-start
  6.5 1.3 collective-permute-start.1
  8.7 3.3 collective-permute-done.1
  12.9 54.7 %gather_fusion = f32[16384,3]{1,0:T(8,128)} fusion(f32[3,5120]{0,1:T(8,128)S(1)} %copy.121, s32[16384]{0:T(1024)S(1)} %broadcast_clamp_fusion), kind=kCustom, calls=%fused_computation | custom fusion | bytes 458752 | tf_op jit(solution)/shard_map/gather | solution.py:40
  67.6 5.2 copy.122
  73.2 4.6 copy.123
  77.8 88.3 %scatter_custom_fusion = f32[3,5120]{0,1:T(8,128)S(1)} fusion(s32[16384]{0:T(1024)S(1)} %bitcast.76, f32[16384,3]{1,0:T(8,128)} %bitcast.70, f32[]{:T(128)} %constant.160.clone.1), kind=kCustom, calls=%fused_computation.21 | custom fusion | flops 49152 | bytes 61952 | tf_op jit(solution)/shard_map/scatter-add | solution.py:45
  166.8 1.3 collective-permute-start.2
  168.8 1.5 slice.203
  170.4 2.2 copy.152
  172.7 4.5 collective-permute-start.3
  177.3 1.3 collective-permute-done.3
  180.0 4.2 collective-permute-start.4
  184.1 1.3 collective-permute-start.5
  185.5 4.2 collective-permute-done.5
  190.5 54.7 %gather_fusion.1 = f32[16384,3]{1,0:T(8,128)} fusion(f32[3,5120]{0,1:T(8,128)S(1)} %copy.128, s32[16384]{0:T(1024)S(1)} %broadcast_clamp_fusion), kind=kCustom, calls=%fused_computation.1 | custom fusion | bytes 458752 | tf_op jit(solution)/shard_map/gather | solution.py:40
  245.3 5.2 copy.129
  250.8 4.6 copy.130
  255.4 88.2 %scatter_custom_fusion.1 = f32[3,5120]{0,1:T(8,128)S(1)} fusion(s32[16384]{0:T(1024)} %bitcast.77, f32[16384,3]{1,0:T(8,128)} %bitcast.71, f32[]{:T(128)} %constant.160.clone.1), kind=kCustom, calls=%fused_computation.19 | custom fusion | flops 49152 | bytes 61952 | tf_op jit(solution)/shard_map/scatter-add | solution.py:45
  344.4 1.3 collective-permute-start.6
  345.7 2.2 copy.142
  347.9 3.5 gather_fusion.3
  351.4 1.5 slice.210
  352.9 2.3 copy.156
  355.4 4.5 collective-permute-start.7
  360.0 1.3 collective-permute-done.7
  362.7 5.0 collective-permute-start.8
  367.7 1.5 collective-permute-start.9
  369.4 5.1 collective-permute-done.9
  375.3 54.7 %gather_fusion.2 = f32[16384,3]{1,0:T(8,128)} fusion(f32[3,5120]{0,1:T(8,128)S(1)} %copy.135, s32[16384]{0:T(1024)S(1)} %broadcast_clamp_fusion), kind=kCustom, calls=%fused_computation.2 | custom fusion | bytes 458752 | tf_op jit(solution)/shard_map/gather | solution.py:40
  430.0 5.2 copy.136
  435.6 4.6 copy.137
  440.2 88.2 %scatter_custom_fusion.2 = f32[3,5120]{0,1:T(8,128)S(1)} fusion(s32[16384]{0:T(1024)} %bitcast.78, f32[16384,3]{1,0:T(8,128)} %bitcast.69, f32[]{:T(128)} %constant.160.clone.1), kind=kCustom, calls=%fused_computation.17 | custom fusion | flops 49152 | bytes 61952 | tf_op jit(solution)/shard_map/scatter-add | solution.py:45
  528.6 1.3 collective-permute-start.10
  530.1 1.5 slice.217
  531.6 2.2 copy.160
  534.0 6.1 collective-permute-start.11
  540.1 1.3 collective-permute-done.11
  542.1 5.4 collective-permute-start.12
  547.5 1.3 collective-permute-start.13
  550.1 4.2 collective-permute-done.13
  554.3 2.3 copy.144
  556.6 22.8 %gather_fusion.4 = f32[6144,3]{1,0:T(8,128)} fusion(f32[3,5120]{0,1:T(8,128)} %copy.144, s32[6144]{0:T(1024)S(1)} %broadcast_clamp_fusion.1), kind=kCustom, calls=%fused_computation.4 | custom fusion | bytes 172032 | tf_op jit(solution)/shard_map/gather | solution.py:69
  579.4 6.9 %copy.145 = f32[8,768,3]{0,2,1:T(4,128)} copy(f32[8,768,3]{2,1,0:T(8,128)} %bitcast.72) | data formatting | bytes 147456 | tf_op jit(solution)/shard_map/gather | solution.py:69
  586.4 8.7 %multiply_bitcast_fusion = f32[3,8,768]{1,0,2:T(4,128)} fusion(f32[8,8,768]{1,0,2:T(8,128)S(1)} %copy.146, f32[8,768,3]{0,2,1:T(4,128)} %copy.145, f32[768]{0:T(1024)S(1)} %fusion.26), kind=kOutput, calls=%fused_computation.16 | convolution fusion | flops 1787904 | bytes 347136 | tf_op jit(solution)/shard_map/ijs,cjs->cis/dot_general | solution.py:70
  595.0 1.9 reshape.290
  598.0 29.3 %all-to-all-start = ((f32[32,1,576]{2,1,0:T(1,128)}), f32[32,1,576]{2,1,0:T(1,128)S(1)}, u32[]{:S(2)}, u32[]{:S(2)}) async-start(f32[32,1,576]{2,1,0:T(1,128)} %reshape.298), calls=%async_computation | async-start | bytes 163840 | tf_op jit(solution)/shard_map/all_to_all | solution.py:77
  627.3 7.7 %all-to-all-done = f32[32,1,576]{2,1,0:T(1,128)S(1)} async-done(((f32[32,1,576]{2,1,0:T(1,128)}), f32[32,1,576]{2,1,0:T(1,128)S(1)}, u32[]{:S(2)}, u32[]{:S(2)}) %all-to-all-start) | async-done | bytes 73760 | tf_op jit(solution)/shard_map/all_to_all | solution.py:77
  (100 shorter events, 17.1 us)
Async XLA Ops:
  0.6 72.2 %copy-start = (f32[24,24]{1,0:T(8,128)S(1)}, f32[24,24]{1,0:T(8,128)}, u32[]{:S(2)}) copy-start(f32[24,24]{1,0:T(8,128)} %param.23) | copy-start | bytes 6916
  1.6 7.1 %collective-permute-start = (f32[3,512]{1,0:T(4,128)S(1)}, f32[3,512]{1,0:T(4,128)S(1)}, u32[]{:S(2)}, u32[]{:S(2)}) collective-permute-start(f32[3,512]{1,0:T(4,128)S(1)} %get-tuple-element.104), channel_id=1, source_target_pairs={{0,1},{1,2},{2,3},{3,4},{4,5},{5,6},{6,7},{7,8},{8,9},{9,10},{10,1... | collective-permute-start | bytes 18440 | tf_op jit(solution)/shard_map/ppermute | solution.py:22
  6.5 5.5 collective-permute-start.1
  8.7 69.1 %copy-start.7 = (s32[1,16,8,128]{3,1,2,0:T(8,128)}, s32[1,16,8,128]{3,1,2,0:T(8,128)S(1)}, u32[]{:S(2)}) copy-start(s32[1,16,8,128]{3,1,2,0:T(8,128)S(1)} %copy.164) | copy-start | bytes 196612
  67.6 5.3 copy-start.11
  166.8 10.5 %collective-permute-start.2 = (f32[3,512]{1,0:T(4,128)}, f32[3,512]{1,0:T(4,128)S(1)}, u32[]{:S(2)}, u32[]{:S(2)}) collective-permute-start(f32[3,512]{1,0:T(4,128)} %copy.154), channel_id=1, source_target_pairs={{1,0},{2,1},{3,2},{4,3},{5,4},{6,5},{7,6},{8,7},{9,8},{10,9},{11,1... | collective-permute-start | bytes 18440 | tf_op jit(solution)/shard_map/ppermute | solution.py:31
  168.8 10.5 %copy-start.3 = (f32[3,4096]{1,0:T(4,128)S(1)}, f32[3,4096]{1,0:T(4,128)}, u32[]{:S(2)}) copy-start(f32[3,4096]{1,0:T(4,128)} %param.22) | copy-start | bytes 147460
  168.8 10.5 %copy-start.6 = (f32[3,4096]{1,0:T(4,128)S(1)}, f32[3,4096]{1,0:T(4,128)}, u32[]{:S(2)}) copy-start(f32[3,4096]{1,0:T(4,128)} %param.21) | copy-start | bytes 147460
  168.8 16.7 %copy-start.14 = (s32[768]{0:T(1024)S(1)}, s32[768]{0:T(1024)}, u32[]{:S(2)}) copy-start(s32[768]{0:T(1024)} %param.26) | copy-start | bytes 9220
  172.7 5.9 collective-permute-start.3
  180.0 70.5 %copy-start.1 = (f32[3,4096]{1,0:T(4,128)}, f32[3,4096]{1,0:T(4,128)S(1)}, u32[]{:S(2)}) copy-start(f32[3,4096]{1,0:T(4,128)S(1)} %get-tuple-element.87) | copy-start | bytes 147460
  180.0 5.5 collective-permute-start.4
  184.1 5.5 collective-permute-start.5
  245.2 5.3 copy-start.12
  344.4 15.5 %collective-permute-start.6 = (f32[3,512]{1,0:T(4,128)}, f32[3,512]{1,0:T(4,128)S(1)}, u32[]{:S(2)}, u32[]{:S(2)}) collective-permute-start(f32[3,512]{1,0:T(4,128)} %copy.158), channel_id=1, source_target_pairs={{1,0},{2,1},{3,2},{4,3},{5,4},{6,5},{7,6},{8,7},{9,8},{10,9},{11,1... | collective-permute-start | bytes 18440 | tf_op jit(solution)/shard_map/ppermute | solution.py:31
  351.4 10.5 %copy-start.2 = (f32[3,4096]{1,0:T(4,128)S(1)}, f32[3,4096]{1,0:T(4,128)}, u32[]{:S(2)}) copy-start(f32[3,4096]{1,0:T(4,128)} %copy-done.1) | copy-start | bytes 147460
  351.4 10.5 %copy-start.4 = (f32[3,4096]{1,0:T(4,128)S(1)}, f32[3,4096]{1,0:T(4,128)}, u32[]{:S(2)}) copy-start(f32[3,4096]{1,0:T(4,128)} %param.22) | copy-start | bytes 147460
  352.9 9.1 %copy-start.9 = (f32[3,4096]{1,0:T(4,128)S(1)}, f32[3,4096]{1,0:T(4,128)}, u32[]{:S(2)}) copy-start(f32[3,4096]{1,0:T(4,128)} %get-tuple-element.88) | copy-start | bytes 147460
  352.9 16.3 %copy-start.5 = (s32[768,8]{1,0:T(8,128)S(1)}, s32[768,8]{1,0:T(8,128)}, u32[]{:S(2)}) copy-start(s32[768,8]{1,0:T(8,128)} %gather_fusion.3) | copy-start | bytes 73732
  355.4 5.9 collective-permute-start.7
  362.7 6.7 %collective-permute-start.8 = (f32[3,512]{1,0:T(4,128)S(1)}, f32[3,512]{1,0:T(4,128)S(1)}, u32[]{:S(2)}, u32[]{:S(2)}) collective-permute-start(f32[3,512]{1,0:T(4,128)S(1)} %get-tuple-element.100), channel_id=1, source_target_pairs={{0,1},{1,2},{2,3},{3,4},{4,5},{5,6},{6,7},{7,8},{8,9},{9,10},{10,1... | collective-permute-start | bytes 18440 | tf_op jit(solution)/shard_map/ppermute | solution.py:22
  367.7 6.8 %collective-permute-start.9 = (f32[3,512]{1,0:T(4,128)S(1)}, f32[3,512]{1,0:T(4,128)S(1)}, u32[]{:S(2)}, u32[]{:S(2)}) collective-permute-start(f32[3,512]{1,0:T(4,128)S(1)} %get-tuple-element.101), channel_id=1, source_target_pairs={{1,0},{2,1},{3,2},{4,3},{5,4},{6,5},{7,6},{8,7},{9,8},{10,9},{11,1... | collective-permute-start | bytes 18440 | tf_op jit(solution)/shard_map/ppermute | solution.py:23
  430.0 5.3 copy-start.13
  440.2 89.7 %copy-start.16 = (s32[1,32]{1,0:T(1,128)S(1)}, s32[1,32]{1,0:T(1,128)}, u32[]{:S(2)}) copy-start(s32[1,32]{1,0:T(1,128)} %param.28) | copy-start | bytes 388
  528.6 11.5 %collective-permute-start.10 = (f32[3,512]{1,0:T(4,128)S(1)}, f32[3,512]{1,0:T(4,128)S(1)}, u32[]{:S(2)}, u32[]{:S(2)}) collective-permute-start(f32[3,512]{1,0:T(4,128)S(1)} %copy.162), channel_id=1, source_target_pairs={{1,0},{2,1},{3,2},{4,3},{5,4},{6,5},{7,6},{8,7},{9,8},{10,9},{11,1... | collective-permute-start | bytes 18440 | tf_op jit(solution)/shard_map/ppermute | solution.py:31
  530.1 12.0 %copy-start.8 = (f32[3,4096]{1,0:T(4,128)S(1)}, f32[3,4096]{1,0:T(4,128)}, u32[]{:S(2)}) copy-start(f32[3,4096]{1,0:T(4,128)} %get-tuple-element.86) | copy-start | bytes 147460
  530.1 18.8 %copy-start.10 = (f32[8,8,768]{2,1,0:T(8,128)S(1)}, f32[8,8,768]{2,1,0:T(8,128)}, u32[]{:S(2)}) copy-start(f32[8,8,768]{2,1,0:T(8,128)} %param.27) | copy-start | bytes 589828
  534.0 7.4 %collective-permute-start.11 = (f32[3,512]{1,0:T(4,128)S(1)}, f32[3,512]{1,0:T(4,128)S(1)}, u32[]{:S(2)}, u32[]{:S(2)}) collective-permute-start(f32[3,512]{1,0:T(4,128)S(1)} %copy.163), channel_id=1, source_target_pairs={{0,1},{1,2},{2,3},{3,4},{4,5},{5,6},{6,7},{7,8},{8,9},{9,10},{10,1... | collective-permute-start | bytes 18440 | tf_op jit(solution)/shard_map/ppermute | solution.py:31
  542.1 8.0 %collective-permute-start.12 = (f32[3,512]{1,0:T(4,128)S(1)}, f32[3,512]{1,0:T(4,128)S(1)}, u32[]{:S(2)}, u32[]{:S(2)}) collective-permute-start(f32[3,512]{1,0:T(4,128)S(1)} %get-tuple-element.98), channel_id=1, source_target_pairs={{0,1},{1,2},{2,3},{3,4},{4,5},{5,6},{6,7},{7,8},{8,9},{9,10},{10,1... | collective-permute-start | bytes 18440 | tf_op jit(solution)/shard_map/ppermute | solution.py:22
  547.5 6.8 %collective-permute-start.13 = (f32[3,512]{1,0:T(4,128)S(1)}, f32[3,512]{1,0:T(4,128)S(1)}, u32[]{:S(2)}, u32[]{:S(2)}) collective-permute-start(f32[3,512]{1,0:T(4,128)S(1)} %get-tuple-element.99), channel_id=1, source_target_pairs={{1,0},{2,1},{3,2},{4,3},{5,4},{6,5},{7,6},{8,7},{9,8},{10,9},{11,1... | collective-permute-start | bytes 18440 | tf_op jit(solution)/shard_map/ppermute | solution.py:23
  595.0 32.2 %copy-start.15 = (s32[1,768]{1,0:T(1,128)S(1)}, s32[1,768]{1,0:T(1,128)}, u32[]{:S(2)}) copy-start(s32[1,768]{1,0:T(1,128)} %param.29) | copy-start | bytes 9220
  598.0 37.0 %all-to-all-start = ((f32[32,1,576]{2,1,0:T(1,128)}), f32[32,1,576]{2,1,0:T(1,128)S(1)}, u32[]{:S(2)}, u32[]{:S(2)}) async-start(f32[32,1,576]{2,1,0:T(1,128)} %reshape.298), calls=%async_computation | async-start | bytes 163840 | tf_op jit(solution)/shard_map/all_to_all | solution.py:77
where the time goes:
time: 639 us; the launch traced here: 638 us
  other arithmetic  272 us (43%)
  local copies, waits for them, and re-layouts  253 us (40%)
  starting transfers between devices  73.2 us (11%)
  waiting for transfers between devices  28.5 us (4%)
  matrix products  10.5 us (2%)
    scatter-add x3, other arithmetic, apply_operator(): jnp.zeros(wide.shape, jnp.float32).at[:, conn]  265 us
    gather x6, local copies, waits for them, and re-layouts, apply_operator(): local = wide[:, conn].reshape(24, -1)  180 us
    gather x3, local copies, waits for them, and re-layouts, on_device(): values = wide[:, conn[:, felem]]  33.2 us
    all_to_all x1, starting transfers between devices, on_device(): lax.all_to_all(contrib, ('fine', 'coarse'), split_axis=1, concat_axis=1,...  29.3 us
    ppermute x4, starting transfers between devices, with_halo(): before = lax.ppermute(last, axis, up)  19.5 us
    ppermute x6, starting transfers between devices, shifted(): lax.ppermute(value, axis, [(source, source + steps) for source in range(f...  19 us
    ppermute x4, waiting for transfers between devices, with_halo(): after = lax.ppermute(first, axis, down)  16.8 us
    reshape x3, local copies, waits for them, and re-layouts, apply_operator(): product.reshape(3, 8, -1)  13.7 us
  transfers between devices with their start and end apart: 15, of which 8 were waited for; matrix products, arithmetic and copies ran while one was open for 3% of the time, Pallas kernels for 0%

commit v1 on v0

v1 whole, which is shorter than its diff:
```python
import functools

import jax
import jax.numpy as jnp
from jax import lax
from jax.experimental import pallas as pl
from jax.experimental.pallas import tpu as pltpu
from jax.sharding import PartitionSpec as P

BAND = 512
CAP = 24
CE_DEV = 128
LOW_END = 0.3
HIGH_END = 2.5
SWEEPS = 3
LANES = 128
ROW = 256
SPACE = 32
GROUP = 16
TILES = 4

THETA = (HIGH_END + LOW_END) / 2.0
DELTA = (HIGH_END - LOW_END) / 2.0
SIGMA = THETA / DELTA


def schedule():
    rho = 1.0 / SIGMA
    steps = []
    for _ in range(SWEEPS - 1):
        rho_new = 1.0 / (2.0 * SIGMA - rho)
        steps.append((rho_new * rho, 2.0 * rho_new / DELTA))
        rho = rho_new
    return steps + [(0.0, 0.0)]


def split(value):
    high = value.astype(jnp.bfloat16).astype(jnp.float32)
    return (high, value - high)


def pick(row, index):
    table = jnp.broadcast_to(row, index.shape)
    return jnp.take_along_axis(table, index, axis=1, mode="promise_in_bounds")


def spread(tiles, lane, local):
    first, at = divmod(local * CAP, LANES)
    out = None
    for c, row in enumerate(tiles):
        piece = pltpu.roll(row[first], (c * SPACE - at) % LANES, axis=1)
        left = LANES - at
        if left < CAP:
            rest = pltpu.roll(row[first + 1], (c * SPACE + left) % LANES, axis=1)
            piece = jnp.where(lane < c * SPACE + left, piece, rest)
        out = piece if c == 0 else jnp.where(lane < c * SPACE, out, piece)
    return out


def kernel(
    sizes, force, inv_diag, k_ref, coefs, conn, felem, weights, counts, celem,
    smoothed, load,
    direction, resid, scale, total, part, local, onehot, slot_node, values, contrib,
    sent, selector, arrived, stacked, snd, rcv,
    snd_sem, rcv_sem, out_sem, in_sem, own_sem,
):
    fine, coarse = sizes
    devices = fine * coarse
    me = lax.axis_index("fine") * coarse + lax.axis_index("coarse")
    nodes = force.shape[1]
    owned = nodes // ROW
    edge = BAND // ROW
    rows = owned + 2 * edge
    stride = total.shape[0] // 3
    elems = conn.shape[1]
    slots = felem.shape[1]
    window = 2 * edge

    def place(index):
        return (index // coarse, lax.rem(index, coarse))

    barrier = pltpu.get_barrier_semaphore()

    @pl.loop(1, devices)
    def _(step):
        pl.semaphore_signal(
            barrier, inc=1, device_id=place(lax.rem(me + step, devices)),
            device_id_type=pl.DeviceIdType.MESH,
        )

    resid[...] = jnp.zeros_like(resid)
    scale[...] = jnp.zeros_like(scale)
    for c in range(3):
        for h in range(owned):
            at = c * stride + edge + h
            resid[at : at + 1, :] = force[c : c + 1, h * ROW : (h + 1) * ROW]
            scale[at : at + 1, :] = inv_diag[c : c + 1, h * ROW : (h + 1) * ROW]
    for d, begin in enumerate((edge, owned)):
        for a, field in enumerate((resid, scale)):
            for c in range(3):
                at = c * stride + begin
                to = (a * 3 + c) * edge
                snd[0, d, to : to + edge, :] = field[at : at + edge, :]

    @pl.loop(0, 8)
    def _(j):
        low = jnp.bitwise_and(conn[pl.ds(j, 1), :], ROW - 1)
        hit = lax.broadcasted_iota(jnp.int32, (ROW, elems), 0) == low
        onehot[j] = jnp.where(hit, 1.0, 0.0).astype(jnp.bfloat16)

    @pl.loop(0, slots // LANES)
    def _(tile):
        at = pl.multiple_of(tile * LANES, LANES)
        element = jnp.broadcast_to(felem[:, pl.ds(at, LANES)], (8, LANES))
        low = jnp.bitwise_and(element, LANES - 1)
        high = lax.shift_right_logical(element, 7)
        found = jnp.zeros((8, LANES), jnp.int32)
        for t in range(elems // LANES):
            got = jnp.take_along_axis(
                conn[:, t * LANES : (t + 1) * LANES], low, axis=1, mode="promise_in_bounds"
            )
            found = jnp.where(high == t, got, found)
        slot_node[:, pl.ds(at, LANES)] = found

    lane = lax.broadcasted_iota(jnp.int32, (8, LANES), 1)
    coarse_iota = lax.broadcasted_iota(jnp.int32, (CE_DEV, LANES), 0)
    group_tiles = GROUP * CAP // LANES

    @pl.loop(0, devices // GROUP)
    def _(group):
        base = group * (GROUP * CAP)
        ids = [
            jnp.broadcast_to(
                celem[:, pl.ds(pl.multiple_of(base + t * LANES, LANES), LANES)], (8, LANES)
            )
            for t in range(group_tiles)
        ]
        for o in range(GROUP):
            owner = spread([ids, ids, ids], lane, o)
            hit = coarse_iota == owner[0:1, :]
            at = pl.multiple_of((group * GROUP + o) * LANES, LANES)
            selector[:, pl.ds(at, LANES)] = jnp.where(hit, 1.0, 0.0).astype(jnp.bfloat16)

    pl.semaphore_wait(barrier, devices - 1)

    lower, upper = (place(lax.rem(me + devices - 1, devices)), place(lax.rem(me + 1, devices)))

    def edge_copy(phase, d, target):
        return pltpu.make_async_remote_copy(
            src_ref=snd.at[phase, d],
            dst_ref=rcv.at[phase, d],
            send_sem=snd_sem.at[phase, d],
            recv_sem=rcv_sem.at[phase, d],
            device_id=target,
            device_id_type=pl.DeviceIdType.MESH,
        )

    def exchange(phase):
        down, up = edge_copy(phase, 0, lower), edge_copy(phase, 1, upper)

        @pl.when(me > 0)
        def _():
            down.start()

        @pl.when(me < devices - 1)
        def _():
            up.start()

        @pl.when(me > 0)
        def _():
            up.wait_recv()
            down.wait_send()

        @pl.when(me < devices - 1)
        def _():
            down.wait_recv()
            up.wait_send()

    exchange(0)

    @pl.when(me > 0)
    def _():
        for a, field in enumerate((resid, scale)):
            for c in range(3):
                at, to = (c * stride, (a * 3 + c) * edge)
                field[at : at + edge, :] = rcv[0, 1, to : to + edge, :]

    @pl.when(me < devices - 1)
    def _():
        for a, field in enumerate((resid, scale)):
            for c in range(3):
                at, to = (c * stride + edge + owned, (a * 3 + c) * edge)
                field[at : at + edge, :] = rcv[0, 0, to : to + edge, :]

    direction[...] = scale[...] * resid[...] / THETA
    total[...] = jnp.zeros_like(total)

    def gather(field, index, count):
        low = [jnp.bitwise_and(i, LANES - 1) for i in index]
        high = [lax.shift_right_logical(i, 7) for i in index]
        out = [[jnp.zeros((8, LANES), jnp.float32) for _ in range(count)] for _ in range(3)]
        for h in range(rows * ROW // LANES):
            at, side = divmod(h, ROW // LANES)
            here = [i == h for i in high]
            for c in range(3):
                r = c * stride + at
                row = field[r : r + 1, side * LANES : (side + 1) * LANES]
                for t in range(count):
                    out[c][t] = jnp.where(here[t], pick(row, low[t]), out[c][t])
        return out

    row_iota = lax.broadcasted_iota(jnp.int32, (stride, elems), 0)
    steps = schedule()

    @pl.loop(0, SWEEPS)
    def _(sweep):
        total[...] += direction[...]

        @pl.loop(0, elems // (LANES * TILES))
        def _(chunk):
            starts = [pl.multiple_of((chunk * TILES + t) * LANES, LANES) for t in range(TILES)]
            index = [conn[:, pl.ds(s, LANES)] for s in starts]
            got = gather(direction, index, TILES)
            for c in range(3):
                for t in range(TILES):
                    local[c * 8 : (c + 1) * 8, pl.ds(starts[t], LANES)] = got[c][t]

        product = (
            jnp.dot(
                k_ref[...], local[...], precision=lax.Precision.HIGHEST,
                preferred_element_type=jnp.float32,
            )
            * coefs[...]
        )
        local[...] = product
        part[...] = jnp.zeros_like(part)

        @pl.loop(0, 8)
        def _(j):
            high = lax.shift_right_logical(conn[pl.ds(j, 1), :], 8)
            hit = row_iota == high
            halves = [split(local[pl.ds(c * 8 + j, 1), :]) for c in range(3)]
            left = jnp.concatenate(
                [jnp.where(hit, halves[c][s], 0.0) for s in range(2) for c in range(3)], axis=0
            ).astype(jnp.bfloat16)
            part[...] += lax.dot_general(
                left, onehot[j], (((1,), (1,)), ((), ())), preferred_element_type=jnp.float32
            )

        both = part[: 3 * stride, :] + part[3 * stride :, :]
        part[: 3 * stride, :] = both
        for d, begin in enumerate((0, owned)):
            for c in range(3):
                at = c * stride + begin
                snd[sweep + 1, d, c * window : (c + 1) * window, :] = part[at : at + window, :]
        exchange(sweep + 1)

        @pl.when(me > 0)
        def _():
            for c in range(3):
                part[c * stride : c * stride + window, :] += rcv[
                    sweep + 1, 1, c * window : (c + 1) * window, :
                ]

        @pl.when(me == 0)
        def _():
            for c in range(3):
                part[c * stride : c * stride + edge, :] = jnp.zeros((edge, ROW), jnp.float32)

        @pl.when(me < devices - 1)
        def _():
            for c in range(3):
                at = c * stride + owned
                part[at : at + window, :] += rcv[sweep + 1, 0, c * window : (c + 1) * window, :]

        @pl.when(me == devices - 1)
        def _():
            for c in range(3):
                at = c * stride + edge + owned
                part[at : at + edge, :] = jnp.zeros((edge, ROW), jnp.float32)

        new = resid[...] - part[: 3 * stride, :]
        resid[...] = new
        keep = jnp.where(sweep == 0, steps[0][0], steps[1][0])
        add = jnp.where(sweep == 0, steps[0][1], steps[1][1])
        direction[...] = keep * direction[...] + add * scale[...] * new

    @pl.loop(0, slots // LANES)
    def _(tile):
        at = pl.multiple_of(tile * LANES, LANES)
        got = gather(resid, [slot_node[:, pl.ds(at, LANES)]], 1)
        for c in range(3):
            values[c * 8 : (c + 1) * 8, :] = got[c][0]
        for c in range(3):
            acc = jnp.zeros((8, LANES), jnp.float32)
            for j in range(8):
                acc = acc + weights[:, j, pl.ds(at, LANES)] * values[c * 8 + j : c * 8 + j + 1, :]
            contrib[c * 8 : (c + 1) * 8, pl.ds(at, LANES)] = acc

    lane_slot = jnp.bitwise_and(lane, SPACE - 1)

    @pl.loop(0, devices // GROUP)
    def _(group):
        base = group * (GROUP * CAP)
        tiles = [
            [
                contrib[
                    c * 8 : (c + 1) * 8,
                    pl.ds(pl.multiple_of(base + t * LANES, LANES), LANES),
                ]
                for t in range(group_tiles)
            ]
            for c in range(3)
        ]
        for o in range(GROUP):
            owner = group * GROUP + o
            live = (lane_slot < counts[0, owner]) & (lane < 3 * SPACE)
            sent[owner] = jnp.where(live, spread(tiles, lane, o), 0.0)

    def slot_copy(target):
        return pltpu.make_async_remote_copy(
            src_ref=sent.at[target],
            dst_ref=arrived.at[me],
            send_sem=out_sem.at[target],
            recv_sem=in_sem.at[me],
            device_id=place(target),
            device_id_type=pl.DeviceIdType.MESH,
        )

    def slot_arrival(source):
        return pltpu.make_async_remote_copy(
            src_ref=sent.at[source],
            dst_ref=arrived.at[source],
            send_sem=out_sem.at[source],
            recv_sem=in_sem.at[source],
            device_id=place(source),
            device_id_type=pl.DeviceIdType.MESH,
        )

    @pl.loop(1, devices)
    def _(step):
        slot_copy(lax.rem(me + step, devices)).start()

    own = pltpu.make_async_copy(sent.at[me], arrived.at[me], own_sem)
    own.start()

    for c in range(3):
        for h in range(owned):
            at = c * stride + edge + h
            smoothed[c : c + 1, h * ROW : (h + 1) * ROW] = total[at : at + 1, :]

    own.wait()

    @pl.loop(1, devices)
    def _(step):
        slot_arrival(lax.rem(me + step, devices)).wait_recv()

    @pl.loop(0, devices)
    def _(source):
        got = arrived[source]
        pieces = [
            split(jnp.where((lane >= c * SPACE) & (lane < (c + 1) * SPACE), got, 0.0))
            for c in range(3)
        ]
        stacked[:, pl.ds(pl.multiple_of(source * LANES, LANES), LANES)] = jnp.concatenate(
            [pieces[c][s] for s in range(2) for c in range(3)], axis=0
        ).astype(jnp.bfloat16)

    sums = lax.dot_general(
        stacked[...], selector[...], (((1,), (1,)), ((), ())), preferred_element_type=jnp.float32
    )
    load[...] = sums[:24, :] + sums[24:, :]

    @pl.loop(1, devices)
    def _(step):
        slot_copy(lax.rem(me + step, devices)).wait_send()


def on_device(sizes, force, inv_diag, k_ref, coefs, conn, felem, weights, counts, celem):
    devices = sizes[0] * sizes[1]
    nodes = force.shape[1]
    elems = conn.shape[1]
    slots = felem.shape[0]
    rows = (nodes + 2 * BAND) // ROW
    stride = -(-rows // 8) * 8
    edge_rows = 6 * BAND // ROW
    field = pltpu.VMEM((3 * stride, ROW), jnp.float32)
    edges = pltpu.VMEM((SWEEPS + 1, 2, edge_rows, ROW), jnp.float32)
    vmem = pl.BlockSpec(memory_space=pltpu.VMEM)
    smem = pl.BlockSpec(memory_space=pltpu.SMEM)
    return pl.pallas_call(
        functools.partial(kernel, sizes),
        out_shape=(
            jax.ShapeDtypeStruct((3, nodes), jnp.float32),
            jax.ShapeDtypeStruct((24, CE_DEV), jnp.float32),
        ),
        in_specs=[vmem] * 7 + [smem, vmem],
        out_specs=(vmem, vmem),
        scratch_shapes=[
            field,
            field,
            field,
            field,
            pltpu.VMEM((6 * stride, ROW), jnp.float32),
            pltpu.VMEM((24, elems), jnp.float32),
            pltpu.VMEM((8, ROW, elems), jnp.bfloat16),
            pltpu.VMEM((8, slots), jnp.int32),
            pltpu.VMEM((24, LANES), jnp.float32),
            pltpu.VMEM((24, slots), jnp.float32),
            pltpu.VMEM((devices, 8, LANES), jnp.float32),
            pltpu.VMEM((CE_DEV, devices * LANES), jnp.bfloat16),
            pltpu.VMEM((devices, 8, LANES), jnp.float32),
            pltpu.VMEM((48, devices * LANES), jnp.bfloat16),
            edges,
            edges,
            pltpu.SemaphoreType.DMA((SWEEPS + 1, 2)),
            pltpu.SemaphoreType.DMA((SWEEPS + 1, 2)),
            pltpu.SemaphoreType.DMA((devices,)),
            pltpu.SemaphoreType.DMA((devices,)),
            pltpu.SemaphoreType.DMA,
        ],
        compiler_params=pltpu.CompilerParams(
            collective_id=0, has_side_effects=True, vmem_limit_bytes=48 * 1024 * 1024
        ),
    )(force, inv_diag, k_ref, coefs[None, :], conn, felem[None, :], weights, counts, celem)


def solution(mesh):
    both = ("fine", "coarse")
    placed = (
        P(None, both),
        P(None, both),
        P(),
        P(both),
        P(None, both),
        P(both),
        P(None, None, both),
        P(both, None),
        P(both, None),
    )
    sizes = (mesh.shape["fine"], mesh.shape["coarse"])
    return jax.shard_map(
        functools.partial(on_device, sizes),
        mesh=mesh,
        in_specs=placed,
        out_specs=(P(None, both), P(None, both)),
        check_vma=False,
    )
```

time: 639 us -> 69.1 us (0.11)
  other arithmetic: 272 us -> 0 us
  local copies, waits for them, and re-layouts: 253 us -> 6.77 us
  starting transfers between devices: 73.2 us -> 0 us
  Pallas kernels: 0 us -> 61.3 us
  waiting for transfers between devices: 28.5 us -> 0 us
  matrix products: 10.5 us -> 0 us
    scatter-add x9 -> x0, other arithmetic: 267 us -> none  [the longest x3 265 us: apply_operator(): jnp.zeros(wide.shape, jnp.float32).at[:, conn]]
    gather x9 -> x0, local copies, waits for them, and re-layouts: 213 us -> none  [the longest x6 180 us: apply_operator(): local = wide[:, conn].reshape(24, -1)]
    pallas_call x0 -> x1, Pallas kernels: none -> 61.3 us  [on_device(): pl.pallas_call(functools.partial(kernel, sizes), out_shape=(jax.ShapeDtyp...]
    ppermute x14 -> x0, starting transfers between devices: 43.9 us -> none  [the longest x4 19.5 us: with_halo(): before = lax.ppermute(last, axis, up)]
    all_to_all x1 -> x0, starting transfers between devices: 29.3 us -> none  [on_device(): lax.all_to_all(contrib, ('fine', 'coarse'), split_axis=1, concat_axis=1,...]
    ppermute x14 -> x0, waiting for transfers between devices: 20.8 us -> none  [the longest x4 16.8 us: with_halo(): after = lax.ppermute(first, axis, down)]
    reshape x7 -> x0, local copies, waits for them, and re-layouts: 16.1 us -> none  [the longest x3 13.7 us: apply_operator(): product.reshape(3, 8, -1)]
    dot_general x5 -> x0, matrix products: 10.5 us -> none  [the longest x1 8.65 us: on_device(): jnp.einsum('ijs,cjs->cis', weights, values, precision=lax.Precision.HIGHEST)]
  transfers between devices with their start and end apart: 15 -> 0, of which waited for: 8 -> 0; matrix products, arithmetic and copies ran while one was open for 3% -> 0% of each run, Pallas kernels for 0% -> 0%
where the time goes in v1:
time: 69.1 us; the launch traced here: 68.7 us
  Pallas kernels  61.3 us (89%)
  local copies, waits for them, and re-layouts  6.77 us (10%)
    pallas_call x1, Pallas kernels, on_device(): pl.pallas_call(functools.partial(kernel, sizes), out_shape=(jax.ShapeDtyp...  61.3 us
    unnamed x18, local copies, waits for them, and re-layouts  6.07 us

profile of v1, /device:TPU:0, one launch (start us, length us, event | category | flops | bytes accessed | tf_op | source)
XLA Modules:
  0.0 68.7 jit_solution(13858237241075334751)
XLA Ops:
  0.6 0.0 copy-start.5
  0.6 0.0 copy-start.7
  0.7 0.7 %broadcast_in_dim.7.felem = s32[1,768]{1,0:T(1,128)S(1)} reshape(s32[768]{0:T(1024)} %param.14) | data formatting | bytes 6144 | tf_op jit(solution)/shard_map/broadcast_in_dim | solution.py:425
  1.4 0.0 copy-done.5
  1.4 0.0 copy-done.7
  1.4 0.0 copy-start
  1.4 0.9 %copy-done = f32[8,8,768]{2,1,0:T(8,128)S(1)} copy-done((f32[8,8,768]{2,1,0:T(8,128)S(1)}, f32[8,8,768]{2,1,0:T(8,128)}, u32[]{:S(2)}) %copy-start) | copy-done | bytes 196632
  2.3 0.0 copy-start.1
  2.3 0.8 %copy-done.1 = f32[3,4096]{1,0:T(4,128)S(1)} copy-done((f32[3,4096]{1,0:T(4,128)S(1)}, f32[3,4096]{1,0:T(4,128)}, u32[]{:S(2)}) %copy-start.1) | copy-done | bytes 49176
  3.1 0.0 copy-start.2
  3.1 0.8 %copy-done.2 = f32[3,4096]{1,0:T(4,128)S(1)} copy-done((f32[3,4096]{1,0:T(4,128)S(1)}, f32[3,4096]{1,0:T(4,128)}, u32[]{:S(2)}) %copy-start.2) | copy-done | bytes 49176
  4.0 0.0 copy-start.3
  4.0 0.8 %copy-done.3 = s32[8,2048]{1,0:T(8,128)S(1)} copy-done((s32[8,2048]{1,0:T(8,128)S(1)}, s32[8,2048]{1,0:T(8,128)}, u32[]{:S(2)}) %copy-start.3) | copy-done | bytes 65560
  4.8 0.0 copy-start.4
  4.8 0.7 %copy-done.4 = f32[24,24]{1,0:T(8,128)S(1)} copy-done((f32[24,24]{1,0:T(8,128)S(1)}, f32[24,24]{1,0:T(8,128)}, u32[]{:S(2)}) %copy-start.4) | copy-done | bytes 2328
  5.5 0.0 copy-start.6
  5.5 0.7 copy-done.6
  6.2 61.3 %shard_map.104 = (f32[3,4096]{1,0:T(4,128)S(1)}, f32[24,128]{1,0:T(8,128)S(1)}) custom-call(f32[3,4096]{1,0:T(4,128)S(1)} %copy-done.1, f32[3,4096]{1,0:T(4,128)S(1)} %copy-done.2, f32[24,24]{1,0:T(8,128)S(1)} %copy-done.4, f32[1,2048]{1,0:T(1,128)S(1)} %bitcast.1, s32[8,2048]{1,0:T(8,128)S(1)} %copy-done.3, s32[1,768]{1,0:T(1,128)S(1)} %broadcast_in_dim.7.felem, ...), custom_call_target="tpu_custom_call" | custom-call | tf_op jit(solution)/shard_map/pallas_call | solution.py:391
  67.5 0.6 copy.13
  68.1 0.6 copy.14
Async XLA Ops:
  0.6 0.7 %copy-start.5 = (f32[2048]{0:T(1024)S(1)}, f32[2048]{0:T(1024)}, u32[]{:S(2)}) copy-start(f32[2048]{0:T(1024)} %param.12) | copy-start | bytes 24580
  0.6 0.7 %copy-start.7 = (s32[1,32]{1,0:T(1,128)S(1)}, s32[1,32]{1,0:T(1,128)}, u32[]{:S(2)}) copy-start(s32[1,32]{1,0:T(1,128)} %counts.1) | copy-start | bytes 388
  1.4 0.9 %copy-start = (f32[8,8,768]{2,1,0:T(8,128)S(1)}, f32[8,8,768]{2,1,0:T(8,128)}, u32[]{:S(2)}) copy-start(f32[8,8,768]{2,1,0:T(8,128)} %weights.1) | copy-start | bytes 589828
  2.3 0.8 %copy-start.1 = (f32[3,4096]{1,0:T(4,128)S(1)}, f32[3,4096]{1,0:T(4,128)}, u32[]{:S(2)}) copy-start(f32[3,4096]{1,0:T(4,128)} %force.1) | copy-start | bytes 147460
  3.1 0.8 %copy-start.2 = (f32[3,4096]{1,0:T(4,128)S(1)}, f32[3,4096]{1,0:T(4,128)}, u32[]{:S(2)}) copy-start(f32[3,4096]{1,0:T(4,128)} %inv_diag.1) | copy-start | bytes 147460
  4.0 0.8 %copy-start.3 = (s32[8,2048]{1,0:T(8,128)S(1)}, s32[8,2048]{1,0:T(8,128)}, u32[]{:S(2)}) copy-start(s32[8,2048]{1,0:T(8,128)} %conn.1) | copy-start | bytes 196612
  4.8 0.7 %copy-start.4 = (f32[24,24]{1,0:T(8,128)S(1)}, f32[24,24]{1,0:T(8,128)}, u32[]{:S(2)}) copy-start(f32[24,24]{1,0:T(8,128)} %k_ref.1) | copy-start | bytes 6916
  5.5 0.7 copy-start.6

commit v2 on v1

--- a/solution.py
+++ b/solution.py
@@ -17,7 +17,7 @@
 ROW = 256
 SPACE = 32
 GROUP = 16
-TILES = 4
+TILES = 2
 
 THETA = (HIGH_END + LOW_END) / 2.0
 DELTA = (HIGH_END - LOW_END) / 2.0
@@ -58,11 +58,12 @@
 
 
 def kernel(
-    sizes, force, inv_diag, k_ref, coefs, conn, felem, weights, counts, celem,
-    smoothed, load,
+    sizes, force_in, inv_diag_in, k_ref_in, coefs_in, conn_in, felem_in, weights_in, counts,
+    celem_in, smoothed, load,
+    force, inv_diag, k_ref, coefs, conn, felem, weights, celem,
     direction, resid, scale, total, part, local, onehot, slot_node, values, contrib,
     sent, selector, arrived, stacked, snd, rcv,
-    snd_sem, rcv_sem, out_sem, in_sem, own_sem,
+    snd_sem, rcv_sem, out_sem, in_sem, own_sem, load_sem,
 ):
     fine, coarse = sizes
     devices = fine * coarse
@@ -79,6 +80,14 @@
     def place(index):
         return (index // coarse, lax.rem(index, coarse))
 
+    pairs = [
+        (force_in, force), (inv_diag_in, inv_diag), (conn_in, conn), (felem_in, felem.at[0]),
+        (celem_in, celem), (k_ref_in, k_ref), (coefs_in, coefs.at[0]), (weights_in, weights),
+    ]
+    loads = [pltpu.make_async_copy(a, b, load_sem.at[n]) for n, (a, b) in enumerate(pairs)]
+    for copy in loads:
+        copy.start()
+
     barrier = pltpu.get_barrier_semaphore()
 
     @pl.loop(1, devices)
@@ -90,6 +99,8 @@
 
     resid[...] = jnp.zeros_like(resid)
     scale[...] = jnp.zeros_like(scale)
+    loads[0].wait()
+    loads[1].wait()
     for c in range(3):
         for h in range(owned):
             at = c * stride + edge + h
@@ -101,6 +112,9 @@
                 at = c * stride + begin
                 to = (a * 3 + c) * edge
                 snd[0, d, to : to + edge, :] = field[at : at + edge, :]
+
+    for copy in loads[2:5]:
+        copy.wait()
 
     @pl.loop(0, 8)
     def _(j):
@@ -155,7 +169,7 @@
             device_id_type=pl.DeviceIdType.MESH,
         )
 
-    def exchange(phase):
+    def edge_start(phase):
         down, up = edge_copy(phase, 0, lower), edge_copy(phase, 1, upper)
 
         @pl.when(me > 0)
@@ -165,6 +179,9 @@
         @pl.when(me < devices - 1)
         def _():
             up.start()
+
+    def edge_wait(phase):
+        down, up = edge_copy(phase, 0, lower), edge_copy(phase, 1, upper)
 
         @pl.when(me > 0)
         def _():
@@ -176,54 +193,113 @@
             down.wait_recv()
             up.wait_send()
 
-    exchange(0)
-
-    @pl.when(me > 0)
-    def _():
-        for a, field in enumerate((resid, scale)):
+    edge_start(0)
+    for copy in loads[5:]:
+        copy.wait()
+
+    def fill_edges():
+        @pl.when(me > 0)
+        def _():
+            for a, field in enumerate((resid, scale)):
+                for c in range(3):
+                    at, to = (c * stride, (a * 3 + c) * edge)
+                    field[at : at + edge, :] = rcv[0, 1, to : to + edge, :]
+
+        @pl.when(me < devices - 1)
+        def _():
+            for a, field in enumerate((resid, scale)):
+                for c in range(3):
+                    at, to = (c * stride + edge + owned, (a * 3 + c) * edge)
+                    field[at : at + edge, :] = rcv[0, 0, to : to + edge, :]
+
+        direction[...] = scale[...] * resid[...] / THETA
+
+    def add_edges(phase, add):
+        def from_side(d, begin):
             for c in range(3):
-                at, to = (c * stride, (a * 3 + c) * edge)
-                field[at : at + edge, :] = rcv[0, 1, to : to + edge, :]
-
-    @pl.when(me < devices - 1)
-    def _():
-        for a, field in enumerate((resid, scale)):
+                at = slice(c * stride + begin, c * stride + begin + window)
+                theirs = rcv[phase, d, c * window : (c + 1) * window, :]
+                resid[at, :] -= theirs
+                direction[at, :] -= add * scale[at, :] * theirs
+
+        def clear(begin):
             for c in range(3):
-                at, to = (c * stride + edge + owned, (a * 3 + c) * edge)
-                field[at : at + edge, :] = rcv[0, 0, to : to + edge, :]
+                at = c * stride + begin
+                resid[at : at + edge, :] = jnp.zeros((edge, ROW), jnp.float32)
+
+        @pl.when(me > 0)
+        def _():
+            from_side(1, 0)
+
+        @pl.when(me == 0)
+        def _():
+            clear(0)
+
+        @pl.when(me < devices - 1)
+        def _():
+            from_side(0, owned)
+
+        @pl.when(me == devices - 1)
+        def _():
+            clear(edge + owned)
 
     direction[...] = scale[...] * resid[...] / THETA
     total[...] = jnp.zeros_like(total)
 
-    def gather(field, index, count):
+    per_row = ROW // LANES
+    inner = range(window * per_row, owned * per_row)
+    outer = [h for h in range(rows * per_row) if h not in inner]
+
+    def gather(field, index, hs, out):
         low = [jnp.bitwise_and(i, LANES - 1) for i in index]
         high = [lax.shift_right_logical(i, 7) for i in index]
-        out = [[jnp.zeros((8, LANES), jnp.float32) for _ in range(count)] for _ in range(3)]
-        for h in range(rows * ROW // LANES):
-            at, side = divmod(h, ROW // LANES)
+        for h in hs:
+            at, side = divmod(h, per_row)
             here = [i == h for i in high]
             for c in range(3):
                 r = c * stride + at
                 row = field[r : r + 1, side * LANES : (side + 1) * LANES]
-                for t in range(count):
+                for t in range(len(index)):
                     out[c][t] = jnp.where(here[t], pick(row, low[t]), out[c][t])
         return out
 
-    row_iota = lax.broadcasted_iota(jnp.int32, (stride, elems), 0)
-    steps = schedule()
-
-    @pl.loop(0, SWEEPS)
-    def _(sweep):
-        total[...] += direction[...]
-
+    def gather_local(hs, first):
         @pl.loop(0, elems // (LANES * TILES))
         def _(chunk):
             starts = [pl.multiple_of((chunk * TILES + t) * LANES, LANES) for t in range(TILES)]
             index = [conn[:, pl.ds(s, LANES)] for s in starts]
-            got = gather(direction, index, TILES)
+            out = [
+                [
+                    jnp.zeros((8, LANES), jnp.float32)
+                    if first
+                    else local[c * 8 : (c + 1) * 8, pl.ds(starts[t], LANES)]
+                    for t in range(TILES)
+                ]
+                for c in range(3)
+            ]
+            got = gather(direction, index, hs, out)
             for c in range(3):
                 for t in range(TILES):
                     local[c * 8 : (c + 1) * 8, pl.ds(starts[t], LANES)] = got[c][t]
+
+    row_iota = lax.broadcasted_iota(jnp.int32, (stride, elems), 0)
+    steps = schedule()
+
+    @pl.loop(0, SWEEPS)
+    def _(sweep):
+        gather_local(inner, True)
+        edge_wait(sweep)
+
+        @pl.when(sweep == 0)
+        def _():
+            fill_edges()
+
+        @pl.when(sweep > 0)
+        def _():
+            add_edges(sweep, jnp.where(sweep == 1, steps[0][1], steps[1][1]))
+
+        total[...] += direction[...]
+        gather_local(outer, False)
 
         product = (
             jnp.dot(
@@ -235,7 +311,7 @@
         local[...] = product
         part[...] = jnp.zeros_like(part)
 
-        @pl.loop(0, 8)
+        @pl.loop(0, 8, unroll=True)
         def _(j):
             high = lax.shift_right_logical(conn[pl.ds(j, 1), :], 8)
             hit = row_iota == high
@@ -253,32 +329,7 @@
             for c in range(3):
                 at = c * stride + begin
                 snd[sweep + 1, d, c * window : (c + 1) * window, :] = part[at : at + window, :]
-        exchange(sweep + 1)
-
-        @pl.when(me > 0)
-        def _():
-            for c in range(3):
-                part[c * stride : c * stride + window, :] += rcv[
-                    sweep + 1, 1, c * window : (c + 1) * window, :
-                ]
-
-        @pl.when(me == 0)
-        def _():
-            for c in range(3):
-                part[c * stride : c * stride + edge, :] = jnp.zeros((edge, ROW), jnp.float32)
-
-        @pl.when(me < devices - 1)
-        def _():
-            for c in range(3):
-                at = c * stride + owned
-                part[at : at + window, :] += rcv[sweep + 1, 0, c * window : (c + 1) * window, :]
-
-        @pl.when(me == devices - 1)
-        def _():
-            for c in range(3):
-                at = c * stride + edge + owned
-                part[at : at + edge, :] = jnp.zeros((edge, ROW), jnp.float32)
-
+        edge_start(sweep + 1)
         new = resid[...] - part[: 3 * stride, :]
         resid[...] = new
         keep = jnp.where(sweep == 0, steps[0][0], steps[1][0])
@@ -288,7 +339,19 @@
     @pl.loop(0, slots // LANES)
     def _(tile):
         at = pl.multiple_of(tile * LANES, LANES)
-        got = gather(resid, [slot_node[:, pl.ds(at, LANES)]], 1)
+        begun = [[jnp.zeros((8, LANES), jnp.float32)] for _ in range(3)]
+        got = gather(resid, [slot_node[:, pl.ds(at, LANES)]], inner, begun)
+        for c in range(3):
+            contrib[c * 8 : (c + 1) * 8, pl.ds(at, LANES)] = got[c][0]
+
+    edge_wait(SWEEPS)
+    add_edges(SWEEPS, 0.0)
+
+    @pl.loop(0, slots // LANES)
+    def _(tile):
+        at = pl.multiple_of(tile * LANES, LANES)
+        begun = [[contrib[c * 8 : (c + 1) * 8, pl.ds(at, LANES)]] for c in range(3)]
+        got = gather(resid, [slot_node[:, pl.ds(at, LANES)]], outer, begun)
         for c in range(3):
             values[c * 8 : (c + 1) * 8, :] = got[c][0]
         for c in range(3):
@@ -387,6 +450,7 @@
     field = pltpu.VMEM((3 * stride, ROW), jnp.float32)
     edges = pltpu.VMEM((SWEEPS + 1, 2, edge_rows, ROW), jnp.float32)
     vmem = pl.BlockSpec(memory_space=pltpu.VMEM)
+    hbm = pl.BlockSpec(memory_space=pltpu.HBM)
     smem = pl.BlockSpec(memory_space=pltpu.SMEM)
     return pl.pallas_call(
         functools.partial(kernel, sizes),
@@ -394,9 +458,17 @@
             jax.ShapeDtypeStruct((3, nodes), jnp.float32),
             jax.ShapeDtypeStruct((24, CE_DEV), jnp.float32),
         ),
-        in_specs=[vmem] * 7 + [smem, vmem],
+        in_specs=[hbm] * 7 + [smem, hbm],
         out_specs=(vmem, vmem),
         scratch_shapes=[
+            pltpu.VMEM((3, nodes), jnp.float32),
+            pltpu.VMEM((3, nodes), jnp.float32),
+            pltpu.VMEM((24, 24), jnp.float32),
+            pltpu.VMEM((1, elems), jnp.float32),
+            pltpu.VMEM((8, elems), jnp.int32),
+            pltpu.VMEM((1, slots), jnp.int32),
+            pltpu.VMEM((8, 8, slots), jnp.float32),
+            pltpu.VMEM((1, slots), jnp.int32),
             field,
             field,
             field,
@@ -418,11 +490,12 @@
             pltpu.SemaphoreType.DMA((devices,)),
             pltpu.SemaphoreType.DMA((devices,)),
             pltpu.SemaphoreType.DMA,
+            pltpu.SemaphoreType.DMA((8,)),
         ],
         compiler_params=pltpu.CompilerParams(
-            collective_id=0, has_side_effects=True, vmem_limit_bytes=48 * 1024 * 1024
+            collective_id=0, has_side_effects=True, vmem_limit_bytes=64 * 1024 * 1024
         ),
-    )(force, inv_diag, k_ref, coefs[None, :], conn, felem[None, :], weights, counts, celem)
+    )(force, inv_diag, k_ref, coefs, conn, felem, weights, counts, celem)
 
 
 def solution(mesh):

time: 69.1 us -> 48.9 us (0.71)
  Pallas kernels: 61.3 us -> 45.9 us
  local copies, waits for them, and re-layouts: 6.77 us -> 2.09 us
    pallas_call x1, Pallas kernels: 61.3 us -> 45.9 us  [on_device(): pl.pallas_call(functools.partial(kernel, sizes), out_shape=(jax.ShapeDtyp...]
    unnamed x18 -> x4, local copies, waits for them, and re-layouts: 6.07 us -> 2.09 us
    broadcast_in_dim x1 -> x0, local copies, waits for them, and re-layouts: 0.7 us -> none  [on_device(): felem[None, :]]
where the time goes in v2:
time: 48.9 us; the launch traced here: 48.7 us
  Pallas kernels  45.9 us (94%)
  local copies, waits for them, and re-layouts  2.09 us (4%)
  between operations  0.65 us (1%)
    pallas_call x1, Pallas kernels, on_device(): pl.pallas_call(functools.partial(kernel, sizes), out_shape=(jax.ShapeDtyp...  45.9 us
    unnamed x4, local copies, waits for them, and re-layouts  2.09 us

profile of v2, /device:TPU:0, one launch (start us, length us, event | category | flops | bytes accessed | tf_op | source)
XLA Modules:
  0.0 48.7 jit_solution(1358369065841158998)
XLA Ops:
  0.6 45.9 %shard_map.104 = (f32[3,4096]{1,0:T(4,128)}, f32[24,128]{1,0:T(8,128)}) custom-call(f32[3,4096]{1,0:T(4,128)} %force_in.1, f32[3,4096]{1,0:T(4,128)} %inv_diag_in.1, f32[24,24]{1,0:T(8,128)} %k_ref_in.1, f32[2048]{0:T(1024)} %coefs_in.1, s32[8,2048]{1,0:T(8,128)} %conn_in.1, s32[768]{0:T(1024)} %felem_in.1, f32[8,8,768]{2,1,0:T(8,128)} %weights_in.1, ...), custom_call_target="tpu_custom_call" | custom-call | tf_op jit(solution)/shard_map/pallas_call | solution.py:455
  46.6 0.0 copy-start
  46.6 1.5 %copy.13 = f32[3,4096]{1,0:T(4,128)} copy(f32[3,4096]{1,0:T(4,128)} %get-tuple-element.4) | data formatting | bytes 98304
  48.1 0.0 copy-done
  48.1 0.6 %copy.14 = f32[24,128]{1,0:T(8,128)} copy(f32[24,128]{1,0:T(8,128)S(1)} %copy-done) | data formatting | bytes 24576
Async XLA Ops:
  46.6 1.5 %copy-start = (f32[24,128]{1,0:T(8,128)S(1)}, f32[24,128]{1,0:T(8,128)}, u32[]{:S(2)}) copy-start(f32[24,128]{1,0:T(8,128)} %get-tuple-element.5) | copy-start | bytes 36868

commit v3 on v2

--- a/solution.py
+++ b/solution.py
@@ -77,6 +77,18 @@
     slots = felem.shape[1]
     window = 2 * edge
 
+    half = snd.shape[2] // 2
+
+    def put_edge(phase, d, to, value):
+        count = value.shape[0]
+        snd[phase, d, to : to + count, :] = value[:, :LANES]
+        snd[phase, d, half + to : half + to + count, :] = value[:, LANES:]
+
+    def get_edge(phase, d, to, count):
+        return jnp.concatenate(
+            [rcv[phase, d, at : at + count, :] for at in (to, half + to)], axis=1
+        )
+
     def place(index):
         return (index // coarse, lax.rem(index, coarse))
 
@@ -111,18 +123,12 @@
             for c in range(3):
                 at = c * stride + begin
                 to = (a * 3 + c) * edge
-                snd[0, d, to : to + edge, :] = field[at : at + edge, :]
+                put_edge(0, d, to, field[at : at + edge, :])
 
     for copy in loads[2:5]:
         copy.wait()
 
-    @pl.loop(0, 8)
-    def _(j):
-        low = jnp.bitwise_and(conn[pl.ds(j, 1), :], ROW - 1)
-        hit = lax.broadcasted_iota(jnp.int32, (ROW, elems), 0) == low
-        onehot[j] = jnp.where(hit, 1.0, 0.0).astype(jnp.bfloat16)
-
-    @pl.loop(0, slots // LANES)
+    @pl.loop(0, slots // LANES, unroll=2)
     def _(tile):
         at = pl.multiple_of(tile * LANES, LANES)
         element = jnp.broadcast_to(felem[:, pl.ds(at, LANES)], (8, LANES))
@@ -194,6 +200,13 @@
             up.wait_send()
 
     edge_start(0)
+
+    @pl.loop(0, 8)
+    def _(j):
+        low = jnp.bitwise_and(conn[pl.ds(j, 1), :], ROW - 1)
+        hit = lax.broadcasted_iota(jnp.int32, (ROW, elems), 0) == low
+        onehot[j] = jnp.where(hit, 1.0, 0.0).astype(jnp.bfloat16)
+
     for copy in loads[5:]:
         copy.wait()
 
@@ -203,14 +216,14 @@
             for a, field in enumerate((resid, scale)):
                 for c in range(3):
                     at, to = (c * stride, (a * 3 + c) * edge)
-                    field[at : at + edge, :] = rcv[0, 1, to : to + edge, :]
+                    field[at : at + edge, :] = get_edge(0, 1, to, edge)
 
         @pl.when(me < devices - 1)
         def _():
             for a, field in enumerate((resid, scale)):
                 for c in range(3):
                     at, to = (c * stride + edge + owned, (a * 3 + c) * edge)
-                    field[at : at + edge, :] = rcv[0, 0, to : to + edge, :]
+                    field[at : at + edge, :] = get_edge(0, 0, to, edge)
 
         direction[...] = scale[...] * resid[...] / THETA
 
@@ -218,7 +231,7 @@
         def from_side(d, begin):
             for c in range(3):
                 at = slice(c * stride + begin, c * stride + begin + window)
-                theirs = rcv[phase, d, c * window : (c + 1) * window, :]
+                theirs = get_edge(phase, d, c * window, window)
                 resid[at, :] -= theirs
                 direction[at, :] -= add * scale[at, :] * theirs
 
@@ -328,7 +341,7 @@
         for d, begin in enumerate((0, owned)):
             for c in range(3):
                 at = c * stride + begin
-                snd[sweep + 1, d, c * window : (c + 1) * window, :] = part[at : at + window, :]
+                put_edge(sweep + 1, d, c * window, part[at : at + window, :])
         edge_start(sweep + 1)
         new = resid[...] - part[: 3 * stride, :]
         resid[...] = new
@@ -336,7 +349,7 @@
         add = jnp.where(sweep == 0, steps[0][1], steps[1][1])
         direction[...] = keep * direction[...] + add * scale[...] * new
 
-    @pl.loop(0, slots // LANES)
+    @pl.loop(0, slots // LANES, unroll=2)
     def _(tile):
         at = pl.multiple_of(tile * LANES, LANES)
         begun = [[jnp.zeros((8, LANES), jnp.float32)] for _ in range(3)]
@@ -347,7 +360,7 @@
     edge_wait(SWEEPS)
     add_edges(SWEEPS, 0.0)
 
-    @pl.loop(0, slots // LANES)
+    @pl.loop(0, slots // LANES, unroll=2)
     def _(tile):
         at = pl.multiple_of(tile * LANES, LANES)
         begun = [[contrib[c * 8 : (c + 1) * 8, pl.ds(at, LANES)]] for c in range(3)]
@@ -448,7 +461,7 @@
     stride = -(-rows // 8) * 8
     edge_rows = 6 * BAND // ROW
     field = pltpu.VMEM((3 * stride, ROW), jnp.float32)
-    edges = pltpu.VMEM((SWEEPS + 1, 2, edge_rows, ROW), jnp.float32)
+    edges = pltpu.VMEM((SWEEPS + 1, 2, edge_rows * ROW // LANES, LANES), jnp.float32)
     vmem = pl.BlockSpec(memory_space=pltpu.VMEM)
     hbm = pl.BlockSpec(memory_space=pltpu.HBM)
     smem = pl.BlockSpec(memory_space=pltpu.SMEM)

time: 48.9 us -> 48.1 us (0.984)
  Pallas kernels: 45.9 us -> 45.2 us
    pallas_call x1, Pallas kernels: 45.9 us -> 45.2 us  [on_device(): pl.pallas_call(functools.partial(kernel, sizes), out_shape=(jax.ShapeDtyp...]
where the time goes in v3:
time: 48.1 us; the launch traced here: 47.9 us
  Pallas kernels  45.2 us (94%)
  local copies, waits for them, and re-layouts  2.09 us (4%)
  between operations  0.65 us (1%)
    pallas_call x1, Pallas kernels, on_device(): pl.pallas_call(functools.partial(kernel, sizes), out_shape=(jax.ShapeDtyp...  45.2 us
    unnamed x4, local copies, waits for them, and re-layouts  2.09 us

profile of v3, /device:TPU:0, one launch (start us, length us, event | category | flops | bytes accessed | tf_op | source)
XLA Modules:
  0.0 47.9 jit_solution(9209842004049788923)
XLA Ops:
  0.6 45.2 %shard_map.104 = (f32[3,4096]{1,0:T(4,128)}, f32[24,128]{1,0:T(8,128)}) custom-call(f32[3,4096]{1,0:T(4,128)} %force_in.1, f32[3,4096]{1,0:T(4,128)} %inv_diag_in.1, f32[24,24]{1,0:T(8,128)} %k_ref_in.1, f32[2048]{0:T(1024)} %coefs_in.1, s32[8,2048]{1,0:T(8,128)} %conn_in.1, s32[768]{0:T(1024)} %felem_in.1, f32[8,8,768]{2,1,0:T(8,128)} %weights_in.1, ...), custom_call_target="tpu_custom_call" | custom-call | tf_op jit(solution)/shard_map/pallas_call | solution.py:468
  45.8 0.0 copy-start
  45.8 1.5 %copy.13 = f32[3,4096]{1,0:T(4,128)} copy(f32[3,4096]{1,0:T(4,128)} %get-tuple-element.4) | data formatting | bytes 98304
  47.3 0.0 copy-done
  47.3 0.6 %copy.14 = f32[24,128]{1,0:T(8,128)} copy(f32[24,128]{1,0:T(8,128)S(1)} %copy-done) | data formatting | bytes 24576
Async XLA Ops:
  45.8 1.5 %copy-start = (f32[24,128]{1,0:T(8,128)S(1)}, f32[24,128]{1,0:T(8,128)}, u32[]{:S(2)}) copy-start(f32[24,128]{1,0:T(8,128)} %get-tuple-element.5) | copy-start | bytes 36868
